TPU v7x, 128 devices: a whole 4x4x4 slice. The times are simulated.
128 devices in a mesh: seq: 32 (over x, z, core), tp: 4 (over y).
Axes of the slice: x: 4, y: 4, z: 4, core: 2. Of those that a mesh axis runs over, the one named last changes fastest.
Arguments:
- residual: bfloat16 [1024, 2560], P('seq', 'tp'), may hold values from -6 to 6
- queries: bfloat16 [1024, 3072], P('seq', 'tp'), may hold values from -80 to 80
- new_kv: bfloat16 [1024, 512], P('seq'), may hold values from -8 to 8
- cache: bfloat16 [2048, 256, 512], P('seq'), may hold values from -8 to 8
- out_weight: bfloat16 [3072, 2560], P('tp'), may hold values from -0.109375 to 0.109375
- block_counts: int32 [1024], replicated, may hold values from 1 to 8, 2048 in all
- last_fill: int32 [1024], replicated, may hold values from 1 to 256
- block_order: int32 [2048], P('seq'), may hold values from 0 to 2047, each once
Outputs:
- layer_out: bfloat16 [1024, 2560], P('seq', 'tp')
Inputs may be any that keep to these rules, and one draw needn't show every extreme that they name: block_counts sums to 2048, and some request has 8 blocks. last_fill of a request is the live tokens of its last block; all its other blocks are full. block_order is a permutation of the pool entries.
All inputs are finite; a program needn't handle non-finite values.
Results may differ from a plain program's by a relative error of at most 0.012.
Values may be sent and summed in bfloat16 or wider, within the bound.
A program may use at most 256 MiB of HBM per device.

v0:
```python
import jax
import jax.numpy as jnp
from jax import lax
from jax.sharding import PartitionSpec as P

very_low = -1e30


def place_blocks(block_counts, block_order):
    num_req = block_counts.shape[0]
    ends = jnp.cumsum(block_counts)
    pool_start = ends - block_counts
    block_req = jnp.sum((pool_start[None, :] <= block_order[:, None]).astype(jnp.int32), axis=1) - 1
    onehot = block_req[:, None] == jnp.arange(num_req, dtype=jnp.int32)[None, :]
    start_here = jnp.sum(jnp.where(onehot, pool_start[None, :], 0), axis=1)
    count_here = jnp.sum(jnp.where(onehot, block_counts[None, :], 0), axis=1)
    return (block_req, block_order - start_here, count_here, onehot)


def request_table(block_max, block_sum, block_acc, block_req, onehot):
    num_blocks, heads_here, head_dim = block_acc.shape
    num_req = onehot.shape[1]
    same_req = block_req[:, None] == block_req[None, :]
    max_at_block = jnp.max(jnp.where(same_req[:, :, None], block_max[None, :, :], very_low), axis=1)
    factor = jnp.exp(block_max - max_at_block)
    member = onehot.T
    cache_max = jnp.max(jnp.where(member[:, :, None], block_max[None, :, :], very_low), axis=1)
    member_float = member.astype(jnp.float32)
    cache_sum = jnp.dot(member_float, block_sum * factor, precision=lax.Precision.HIGHEST)
    scaled_acc = (block_acc * factor[:, :, None]).reshape(num_blocks, heads_here * head_dim)
    cache_acc = jnp.dot(member_float, scaled_acc, precision=lax.Precision.HIGHEST).reshape(
        num_req, heads_here, head_dim
    )
    return (cache_max, cache_sum, cache_acc)


def local(residual, queries, new_kv, cache, out_weight, block_counts, last_fill, block_order):
    rows_here = residual.shape[0]
    width_here = residual.shape[1]
    head_dim = new_kv.shape[1] // 2
    heads_here = queries.shape[1] // head_dim
    block_len = cache.shape[1]
    num_blocks = cache.shape[0]
    inv_root = 1.0 / head_dim**0.5
    query_all = lax.all_gather(queries, "seq", axis=0, tiled=True)
    block_req, block_slot, count_here, onehot = place_blocks(block_counts, block_order)
    fill_here = jnp.sum(jnp.where(onehot, last_fill[None, :], 0), axis=1)
    live_mask = (block_slot < count_here - 1)[:, None] | (
        jnp.arange(block_len, dtype=jnp.int32)[None, :] < fill_here[:, None]
    )
    query_blocks = query_all[block_req].reshape(num_blocks, heads_here, head_dim)
    keys = cache[:, :, :head_dim]
    values = cache[:, :, head_dim:]
    scores = (
        jnp.einsum("bhd,btd->bht", query_blocks, keys, preferred_element_type=jnp.float32)
        * inv_root
    )
    scores = jnp.where(live_mask[:, None, :], scores, very_low)
    block_max = jnp.max(scores, axis=2)
    weights = jnp.where(live_mask[:, None, :], jnp.exp(scores - block_max[:, :, None]), 0.0)
    block_sum = jnp.sum(weights, axis=2)
    rounded = weights.astype(jnp.bfloat16)
    block_acc = jnp.einsum("bht,btd->bhd", rounded, values, preferred_element_type=jnp.float32)
    cache_max, cache_sum, cache_acc = request_table(
        block_max, block_sum, block_acc, block_req, onehot
    )
    got_max, got_sum, got_acc = (
        lax.all_to_all(cache_max, "seq", split_axis=0, concat_axis=0, tiled=True),
        lax.all_to_all(cache_sum, "seq", split_axis=0, concat_axis=0, tiled=True),
        lax.all_to_all(cache_acc, "seq", split_axis=0, concat_axis=0, tiled=True),
    )
    sources = got_max.shape[0] // rows_here
    got_max = got_max.reshape(sources, rows_here, heads_here)
    got_sum = got_sum.reshape(sources, rows_here, heads_here)
    got_acc = got_acc.reshape(sources, rows_here, heads_here, head_dim)
    home_max = jnp.max(got_max, axis=0)
    source_factor = jnp.exp(got_max - home_max[None, :, :])
    home_sum = jnp.sum(got_sum * source_factor, axis=0)
    home_acc = jnp.sum(got_acc * source_factor[:, :, :, None], axis=0)
    query_home = queries.reshape(rows_here, heads_here, head_dim)
    own_score = (
        jnp.einsum(
            "rhd,rd->rh", query_home, new_kv[:, :head_dim], preferred_element_type=jnp.float32
        )
        * inv_root
    )
    top_score = jnp.maximum(home_max, own_score)
    cache_factor = jnp.exp(home_max - top_score)
    own_factor = jnp.exp(own_score - top_score)
    denominator = home_sum * cache_factor + own_factor
    new_value = new_kv[:, head_dim:].astype(jnp.float32)
    mixed_sum = home_acc * cache_factor[:, :, None] + own_factor[:, :, None] * new_value[:, None, :]
    attention = (
        (mixed_sum / denominator[:, :, None])
        .reshape(rows_here, heads_here * head_dim)
        .astype(jnp.bfloat16)
    )
    partial_out = jnp.dot(attention, out_weight, preferred_element_type=jnp.float32)
    summed = lax.psum(partial_out.astype(jnp.bfloat16), "tp").astype(jnp.float32)
    columns = lax.dynamic_slice_in_dim(summed, lax.axis_index("tp") * width_here, width_here, 1)
    return (residual.astype(jnp.float32) + columns).astype(jnp.bfloat16)


def solution(mesh):
    in_specs = (
        P("seq", "tp"),
        P("seq", "tp"),
        P("seq", None),
        P("seq", None, None),
        P("tp", None),
        P(),
        P(),
        P("seq"),
    )
    out_specs = P("seq", "tp")
    return jax.shard_map(local, mesh=mesh, in_specs=in_specs, out_specs=out_specs, check_vma=False)
```

profile of v0, /device:TPU:0, one launch (start us, length us, event | category | flops | bytes accessed | tf_op | source)
XLA Modules:
  0.0 207.6 jit_solution(12501185500906286605)
XLA Ops:
  6.5 0.0 all-gather.2.cloned.1.call-start
  6.5 0.7 all-gather.2.cloned.1.call-update
  7.3 1.0 reduce-window.9
  8.2 0.1 slice.19
  8.3 0.1 slice_reduce_fusion
  8.4 0.8 bitcast_subtract_fusion
  9.2 0.8 convert_reduce_fusion
  10.1 1.0 select_reduce_fusion.3
  11.1 0.7 add_compare_fusion
  11.7 0.1 broadcast_compare_fusion
  11.8 0.1 fusion.28
  11.9 0.1 iota_compare_fusion
  12.0 43.5 %all-gather.2.cloned.1.call-done = bf16[1024,768]{1,0:T(8,128)(2,1)} async-done(((bf16[32,768]{1,0:T(8,128)(2,1)}), bf16[1024,768]{1,0:T(8,128)(2,1)}) %all-gather.2.cloned.1.call-update) | async-done | bytes 1572880 | tf_op jit(solution)/shard_map/all_gather | solution.py:45
  55.5 2.4 %gather_fusion = bf16[64,768]{1,0:T(8,128)(2,1)S(1)} fusion(bf16[1024,768]{1,0:T(8,128)(2,1)} %all-gather.2.cloned.1.call-done, s32[1024]{0:T(1024)S(1)} %pad_clamp_fusion), kind=kCustom, calls=%fused_computation | custom fusion | bytes 196864 | tf_op jit(solution)/shard_map/gather | solution.py:51
  57.9 5.7 %fusion.42 = (f32[64,3]{1,0:T(8,128)S(1)}, f32[64,3,256]{2,1,0:T(4,128)S(1)}) fusion(bf16[64,3,256]{2,1,0:T(4,128)(2,1)S(1)} %reshape.170, bf16[64,256,512]{2,1,0:T(8,128)(2,1)} %param.11, pred[64,256]{1,0:T(8,128)(4,1)S(1)} %fusion.28), kind=kOutput, calls=%fused_computation.62 | convolution fusion | flops 25313088 | bytes 8700672 | tf_op jit(solution)/shard_map/bhd,btd->bht/dot_general | solution.py:55
  63.6 0.1 copy.54
  63.7 0.3 fusion.20
  64.0 0.1 select_reduce_fusion.4
  64.1 0.1 copy.55
  64.2 4.6 %fusion.8 = f32[64,3,256]{2,1,0:T(4,128)S(1)} fusion(bf16[64,256,512]{2,1,0:T(8,128)(2,1)} %param.11, f32[64,3,256]{2,1,0:T(4,128)S(1)} %get-tuple-element.16, f32[64,3]{1,0:T(8,128)S(1)} %subtract_exponential_fusion, f32[64,3]{1,0:T(8,128)S(1)} %get-tuple-element.15, pred[64,256]{1,0:T(8,128)(4,1)S(1)} %fusion.28), kind=kOutput, calls=%fused_computation.9 | convolution fusion | flops 25362432 | bytes 8799744 | tf_op jit(solution)/shard_map/bht,btd->bhd/dot_general | solution.py:63
  68.9 0.3 fusion.14
  69.1 0.1 all_to_all.18
  69.2 0.7 copy.63
  69.9 5.2 %all-to-all-start.2 = ((f32[32,32,3]{1,2,0:T(4,128)}), f32[32,32,3]{1,2,0:T(4,128)S(1)}, u32[]{:S(2)}, u32[]{:S(2)}) async-start(f32[32,32,3]{1,2,0:T(4,128)} %copy.63), calls=%async_computation.2 | async-start | bytes 131072 | tf_op jit(solution)/shard_map/all_to_all | solution.py:69
  75.1 0.2 select_reduce_fusion
  75.2 0.1 all_to_all.16
  75.3 0.7 copy.59
  76.0 6.6 %all-to-all-done.2 = f32[32,32,3]{1,2,0:T(4,128)S(1)} async-done(((f32[32,32,3]{1,2,0:T(4,128)}), f32[32,32,3]{1,2,0:T(4,128)S(1)}, u32[]{:S(2)}, u32[]{:S(2)}) %all-to-all-start.2) | async-done | bytes 12320 | tf_op jit(solution)/shard_map/all_to_all | solution.py:69
  82.6 3.8 %all-to-all-start.1 = ((f32[32,32,3]{1,2,0:T(4,128)}), f32[32,32,3]{1,2,0:T(4,128)S(1)}, u32[]{:S(2)}, u32[]{:S(2)}) async-start(f32[32,32,3]{1,2,0:T(4,128)} %copy.59), calls=%async_computation.1 | async-start | bytes 131072 | tf_op jit(solution)/shard_map/all_to_all | solution.py:68
  86.5 1.5 fusion.16
  88.0 4.1 %copy.57 = f32[1024,3,256]{2,1,0:T(4,128)} copy(f32[1024,3,256]{2,0,1:T(8,128)S(1)} %fusion.16) | data formatting | bytes 6291456 | tf_op jit(solution)/shard_map/dot_general | solution.py:31
  92.1 1.9 all-to-all-done.1
  94.0 5.7 %all-to-all-start = ((f32[1024,3,256]{2,1,0:T(4,128)}), f32[1024,3,256]{2,1,0:T(4,128)}, u32[]{:S(2)}, u32[]{:S(2)}) async-start(f32[1024,3,256]{2,1,0:T(4,128)} %copy.57), calls=%async_computation | async-start | bytes 8388608 | tf_op jit(solution)/shard_map/all_to_all | solution.py:70
  99.7 0.0 all-reduce.2.cloned.1.call-start
  99.8 0.0 copy-done.1
  99.8 0.0 copy-done.3
  99.8 0.1 fusion.33
  100.0 0.1 copy.67
  100.1 0.1 reduce_max.39
  100.2 52.3 %all-to-all-done = f32[1024,3,256]{2,1,0:T(4,128)} async-done(((f32[1024,3,256]{2,1,0:T(4,128)}), f32[1024,3,256]{2,1,0:T(4,128)}, u32[]{:S(2)}, u32[]{:S(2)}) %all-to-all-start) | async-done | bytes 3145760 | tf_op jit(solution)/shard_map/all_to_all | solution.py:70
  152.5 2.9 %fusion.4 = f32[32,3,256]{2,0,1:T(8,128)S(1)} fusion(f32[32,32,3,256]{3,2,1,0:T(4,128)} %bitcast.7, f32[32,32,3]{1,0,2:T(8,128)S(1)} %get-tuple-element.12), kind=kLoop, calls=%fused_computation.7 | loop fusion | flops 1548288 | bytes 3256320 | tf_op jit(solution)/shard_map/reduce_sum | solution.py:79
  155.4 0.1 fusion.31
  155.5 0.3 copy-done
  155.9 1.4 convolution_convert_fusion
  157.3 0.0 all-reduce.2.cloned.1.call-update
  157.3 42.0 %all-reduce.2.cloned.1.call-done = bf16[32,2560]{1,0:T(8,128)(2,1)} async-done(((bf16[32,2560]{1,0:T(8,128)(2,1)}), bf16[32,2560]{1,0:T(8,128)(2,1)}) %all-reduce.2.cloned.1.call-update) | async-done | bytes 163856 | tf_op jit(solution)/shard_map/psum | solution.py:99
  199.3 0.0 copy-done.2
  199.3 1.4 add_convert_fusion
  (15 shorter events, 0.2 us)
Async XLA Ops:
  6.5 49.0 %all-gather.2.cloned.1.call-start = ((), (), s32[]{:S(2)}) async-start(), calls=%async_computation.3 | async-start | bytes 1622016 | tf_op jit(solution)/shard_map/all_gather | solution.py:45
  69.9 12.7 %all-to-all-start.2 = ((f32[32,32,3]{1,2,0:T(4,128)}), f32[32,32,3]{1,2,0:T(4,128)S(1)}, u32[]{:S(2)}, u32[]{:S(2)}) async-start(f32[32,32,3]{1,2,0:T(4,128)} %copy.63), calls=%async_computation.2 | async-start | bytes 131072 | tf_op jit(solution)/shard_map/all_to_all | solution.py:69
  82.6 11.4 %all-to-all-start.1 = ((f32[32,32,3]{1,2,0:T(4,128)}), f32[32,32,3]{1,2,0:T(4,128)S(1)}, u32[]{:S(2)}, u32[]{:S(2)}) async-start(f32[32,32,3]{1,2,0:T(4,128)} %copy.59), calls=%async_computation.1 | async-start | bytes 131072 | tf_op jit(solution)/shard_map/all_to_all | solution.py:68
  92.1 7.7 %copy-start.1 = (bf16[32,768]{1,0:T(8,128)(2,1)S(1)}, bf16[32,768]{1,0:T(8,128)(2,1)}, u32[]{:S(2)}) copy-start(bf16[32,768]{1,0:T(8,128)(2,1)} %param.9) | copy-start | bytes 147460
  92.1 7.7 %copy-start.3 = (bf16[32,512]{1,0:T(8,128)(2,1)S(1)}, bf16[32,512]{1,0:T(8,128)(2,1)}, u32[]{:S(2)}) copy-start(bf16[32,512]{1,0:T(8,128)(2,1)} %param.10) | copy-start | bytes 98308
  94.0 58.5 %all-to-all-start = ((f32[1024,3,256]{2,1,0:T(4,128)}), f32[1024,3,256]{2,1,0:T(4,128)}, u32[]{:S(2)}, u32[]{:S(2)}) async-start(f32[1024,3,256]{2,1,0:T(4,128)} %copy.57), calls=%async_computation | async-start | bytes 8388608 | tf_op jit(solution)/shard_map/all_to_all | solution.py:70
  99.7 99.6 %all-reduce.2.cloned.1.call-start = ((), (), s32[]{:S(2)}) async-start(), calls=%async_computation.4 | async-start | bytes 327680 | tf_op jit(solution)/shard_map/psum | solution.py:99
  152.5 3.4 %copy-start = (bf16[768,2560]{1,0:T(8,128)(2,1)S(1)}, bf16[768,2560]{1,0:T(8,128)(2,1)}, u32[]{:S(2)}) copy-start(bf16[768,2560]{1,0:T(8,128)(2,1)} %param.12) | copy-start | bytes 11796484
  152.5 46.8 %copy-start.2 = (bf16[32,640]{1,0:T(8,128)(2,1)S(1)}, bf16[32,640]{1,0:T(8,128)(2,1)}, u32[]{:S(2)}) copy-start(bf16[32,640]{1,0:T(8,128)(2,1)} %param.8) | copy-start | bytes 122884
Sparse Core Ops, SparseCore 0:
  9.6 45.8 all-gather.1
  157.5 41.8 all-reduce.1
where the time goes:
time: 208 us
  waiting for transfers between devices  147 us (71%)
  starting transfers between devices  14.8 us (7%)
  matrix products  13.7 us (7%)
  between operations  13.6 us (7%)
  other arithmetic  9.63 us (5%)
  local copies, waits for them, and re-layouts  8.82 us (4%)
    all_to_all x1, waiting for transfers between devices, local(): lax.all_to_all(cache_acc, 'seq', split_axis=0, concat_axis=0, tiled=True)  52.3 us
    all_gather x1, waiting for transfers between devices, local(): query_all = lax.all_gather(queries, 'seq', axis=0, tiled=True)  43.5 us
    psum x1, waiting for transfers between devices, local(): lax.psum(partial_out.astype(jnp.bfloat16), 'tp').astype(jnp.float32)  42 us
    all_to_all x1, waiting for transfers between devices, local(): lax.all_to_all(cache_sum, 'seq', split_axis=0, concat_axis=0, tiled=True)  6.6 us
    dot_general x1, matrix products, local(): jnp.einsum('bhd,btd->bht', query_blocks, keys, preferred_element_type=jnp...  5.73 us
    all_to_all x1, starting transfers between devices, local(): lax.all_to_all(cache_acc, 'seq', split_axis=0, concat_axis=0, tiled=True)  5.73 us
    all_to_all x1, starting transfers between devices, local(): lax.all_to_all(cache_sum, 'seq', split_axis=0, concat_axis=0, tiled=True)  5.18 us
    dot_general x1, matrix products, local(): jnp.einsum('bht,btd->bhd', rounded, values, preferred_element_type=jnp.fl...  4.62 us
  transfers between devices with their start and end apart: 5, of which 5 were waited for; matrix products, arithmetic and copies ran while one was open for 6% of the time, Pallas kernels for 0%

commit v1 on v0

--- a/solution.py
+++ b/solution.py
@@ -42,7 +42,9 @@
     block_len = cache.shape[1]
     num_blocks = cache.shape[0]
     inv_root = 1.0 / head_dim**0.5
-    query_all = lax.all_gather(queries, "seq", axis=0, tiled=True)
+    query_all = jnp.concatenate(
+        lax.all_to_all(jnp.stack([queries] * lax.axis_size("seq")), "seq", 0, 0), axis=0
+    )
     block_req, block_slot, count_here, onehot = place_blocks(block_counts, block_order)
     fill_here = jnp.sum(jnp.where(onehot, last_fill[None, :], 0), axis=1)
     live_mask = (block_slot < count_here - 1)[:, None] | (

time: 208 us -> 190 us (0.913)
  waiting for transfers between devices: 147 us -> 125 us
  starting transfers between devices: 14.8 us -> 21.7 us
  other arithmetic: 9.63 us -> 6.23 us
    all_gather x1 -> x0, waiting for transfers between devices: 43.5 us -> none  [local(): query_all = lax.all_gather(queries, 'seq', axis=0, tiled=True)]
    all_to_all x0 -> x1, waiting for transfers between devices: none -> 21.7 us  [local(): lax.all_to_all(jnp.stack([queries] * lax.axis_size('seq')), 'seq', 0, 0)]
    all_to_all x0 -> x1, starting transfers between devices: none -> 8.24 us  [local(): lax.all_to_all(jnp.stack([queries] * lax.axis_size('seq')), 'seq', 0, 0)]
    another operation x1 -> x2, local copies, waits for them, and re-layouts: 0.12 us -> 2.29 us  [the longest x1 2.17 us: local(): jnp.stack([queries] * lax.axis_size('seq'))]
  transfers between devices with their start and end apart: 5 -> 5, of which waited for: 5 -> 5; matrix products, arithmetic and copies ran while one was open for 6% -> 4% of each run, Pallas kernels for 0% -> 0%
where the time goes in v1:
time: 190 us; the launch traced here: 189 us
  waiting for transfers between devices  125 us (66%)
  starting transfers between devices  21.7 us (11%)
  matrix products  13.7 us (7%)
  between operations  13.6 us (7%)
  local copies, waits for them, and re-layouts  9.34 us (5%)
  other arithmetic  6.23 us (3%)
    all_to_all x1, waiting for transfers between devices, local(): lax.all_to_all(cache_acc, 'seq', split_axis=0, concat_axis=0, tiled=True)  52.3 us
    psum x1, waiting for transfers between devices, local(): lax.psum(partial_out.astype(jnp.bfloat16), 'tp').astype(jnp.float32)  42.2 us
    all_to_all x1, waiting for transfers between devices, local(): lax.all_to_all(jnp.stack([queries] * lax.axis_size('seq')), 'seq', 0, 0)  21.7 us
    all_to_all x1, starting transfers between devices, local(): lax.all_to_all(jnp.stack([queries] * lax.axis_size('seq')), 'seq', 0, 0)  8.24 us
    all_to_all x1, waiting for transfers between devices, local(): lax.all_to_all(cache_sum, 'seq', split_axis=0, concat_axis=0, tiled=True)  6.6 us
    dot_general x1, matrix products, local(): jnp.einsum('bhd,btd->bht', query_blocks, keys, preferred_element_type=jnp...  5.73 us
    all_to_all x1, starting transfers between devices, local(): lax.all_to_all(cache_acc, 'seq', split_axis=0, concat_axis=0, tiled=True)  5.73 us
    dot_general x1, matrix products, local(): jnp.einsum('bht,btd->bhd', rounded, values, preferred_element_type=jnp.fl...  4.62 us
  transfers between devices with their start and end apart: 5, of which 5 were waited for; matrix products, arithmetic and copies ran while one was open for 4% of the time, Pallas kernels for 0%

profile of v1, /device:TPU:0, one launch (start us, length us, event | category | flops | bytes accessed | tf_op | source)
XLA Modules:
  0.0 189.4 jit_solution(5744483446457195897)
XLA Ops:
  6.5 2.2 %stack.2 = bf16[32,32,768]{2,1,0:T(8,128)(2,1)} broadcast(bf16[32,768]{1,0:T(8,128)(2,1)} %param.9), dimensions={1,2} | broadcast | bytes 1622016 | tf_op jit(solution)/shard_map/stack | solution.py:46
  8.7 8.2 %all-to-all-start = ((bf16[32,32,768]{2,1,0:T(8,128)(2,1)}), bf16[32,32,768]{2,1,0:T(8,128)(2,1)S(1)}, u32[]{:S(2)}, u32[]{:S(2)}) async-start(bf16[32,32,768]{2,1,0:T(8,128)(2,1)} %stack.2), calls=%async_computation | async-start | bytes 3145728 | tf_op jit(solution)/shard_map/all_to_all | solution.py:46
  17.0 0.0 copy-done.3
  17.0 0.3 reduce-window.9
  17.3 0.1 slice.19
  17.4 0.1 slice_reduce_fusion
  17.5 0.1 bitcast_subtract_fusion
  17.6 0.0 copy-done.6
  17.6 0.2 convert_reduce_fusion
  17.8 0.0 copy-done.5
  17.8 0.3 select_reduce_fusion.3
  18.1 0.1 broadcast_compare_fusion
  18.1 0.1 fusion.28
  18.2 0.1 iota_compare_fusion
  18.4 21.7 %all-to-all-done = bf16[32,32,768]{2,1,0:T(8,128)(2,1)S(1)} async-done(((bf16[32,32,768]{2,1,0:T(8,128)(2,1)}), bf16[32,32,768]{2,1,0:T(8,128)(2,1)S(1)}, u32[]{:S(2)}, u32[]{:S(2)}) %all-to-all-start) | async-done | bytes 1572896 | tf_op jit(solution)/shard_map/all_to_all | solution.py:46
  40.1 0.7 gather_fusion
  40.9 5.7 %fusion.42 = (f32[64,3]{1,0:T(8,128)S(1)}, f32[64,3,256]{2,1,0:T(4,128)S(1)}) fusion(bf16[64,3,256]{2,1,0:T(4,128)(2,1)S(1)} %reshape.176, bf16[64,256,512]{2,1,0:T(8,128)(2,1)} %param.11, pred[64,256]{1,0:T(8,128)(4,1)S(1)} %fusion.28), kind=kOutput, calls=%fused_computation.62 | convolution fusion | flops 25313088 | bytes 8700672 | tf_op jit(solution)/shard_map/bhd,btd->bht/dot_general | solution.py:57
  46.6 0.1 copy.54
  46.7 0.3 fusion.20
  47.0 0.1 select_reduce_fusion.4
  47.1 0.1 copy.55
  47.2 4.6 %fusion.8 = f32[64,3,256]{2,1,0:T(4,128)S(1)} fusion(bf16[64,256,512]{2,1,0:T(8,128)(2,1)} %param.11, f32[64,3,256]{2,1,0:T(4,128)S(1)} %get-tuple-element.16, f32[64,3]{1,0:T(8,128)S(1)} %subtract_exponential_fusion, f32[64,3]{1,0:T(8,128)S(1)} %get-tuple-element.15, pred[64,256]{1,0:T(8,128)(4,1)S(1)} %fusion.28), kind=kOutput, calls=%fused_computation.9 | convolution fusion | flops 25362432 | bytes 8799744 | tf_op jit(solution)/shard_map/bht,btd->bhd/dot_general | solution.py:65
  51.8 0.3 fusion.14
  52.1 0.1 all_to_all.22
  52.2 0.7 copy.63
  52.8 3.9 %all-to-all-start.3 = ((f32[32,32,3]{1,2,0:T(4,128)}), f32[32,32,3]{1,2,0:T(4,128)S(1)}, u32[]{:S(2)}, u32[]{:S(2)}) async-start(f32[32,32,3]{1,2,0:T(4,128)} %copy.63), calls=%async_computation.3 | async-start | bytes 131072 | tf_op jit(solution)/shard_map/all_to_all | solution.py:71
  56.7 0.2 select_reduce_fusion
  56.9 0.1 all_to_all.20
  57.0 0.7 copy.59
  57.6 6.6 %all-to-all-done.3 = f32[32,32,3]{1,2,0:T(4,128)S(1)} async-done(((f32[32,32,3]{1,2,0:T(4,128)}), f32[32,32,3]{1,2,0:T(4,128)S(1)}, u32[]{:S(2)}, u32[]{:S(2)}) %all-to-all-start.3) | async-done | bytes 12320 | tf_op jit(solution)/shard_map/all_to_all | solution.py:71
  64.2 3.8 %all-to-all-start.2 = ((f32[32,32,3]{1,2,0:T(4,128)}), f32[32,32,3]{1,2,0:T(4,128)S(1)}, u32[]{:S(2)}, u32[]{:S(2)}) async-start(f32[32,32,3]{1,2,0:T(4,128)} %copy.59), calls=%async_computation.2 | async-start | bytes 131072 | tf_op jit(solution)/shard_map/all_to_all | solution.py:70
  68.1 1.5 fusion.16
  69.6 4.1 %copy.57 = f32[1024,3,256]{2,1,0:T(4,128)} copy(f32[1024,3,256]{2,0,1:T(8,128)S(1)} %fusion.16) | data formatting | bytes 6291456 | tf_op jit(solution)/shard_map/dot_general | solution.py:31
  73.7 1.9 %all-to-all-done.2 = f32[32,32,3]{1,2,0:T(4,128)S(1)} async-done(((f32[32,32,3]{1,2,0:T(4,128)}), f32[32,32,3]{1,2,0:T(4,128)S(1)}, u32[]{:S(2)}, u32[]{:S(2)}) %all-to-all-start.2) | async-done | bytes 12320 | tf_op jit(solution)/shard_map/all_to_all | solution.py:70
  75.6 5.7 %all-to-all-start.1 = ((f32[1024,3,256]{2,1,0:T(4,128)}), f32[1024,3,256]{2,1,0:T(4,128)}, u32[]{:S(2)}, u32[]{:S(2)}) async-start(f32[1024,3,256]{2,1,0:T(4,128)} %copy.57), calls=%async_computation.1 | async-start | bytes 8388608 | tf_op jit(solution)/shard_map/all_to_all | solution.py:72
  81.3 0.0 all-reduce.2.cloned.1.call-start
  81.4 0.0 copy-done.1
  81.5 0.1 fusion.33
  81.6 0.1 copy.67
  81.7 0.1 reduce_max.39
  81.8 52.3 %all-to-all-done.1 = f32[1024,3,256]{2,1,0:T(4,128)} async-done(((f32[1024,3,256]{2,1,0:T(4,128)}), f32[1024,3,256]{2,1,0:T(4,128)}, u32[]{:S(2)}, u32[]{:S(2)}) %all-to-all-start.1) | async-done | bytes 3145760 | tf_op jit(solution)/shard_map/all_to_all | solution.py:72
  134.1 2.9 %fusion.4 = f32[32,3,256]{2,0,1:T(8,128)S(1)} fusion(f32[32,32,3,256]{3,2,1,0:T(4,128)} %bitcast.8, f32[32,32,3]{1,0,2:T(8,128)S(1)} %get-tuple-element.12), kind=kLoop, calls=%fused_computation.7 | loop fusion | flops 1548288 | bytes 3256320 | tf_op jit(solution)/shard_map/reduce_sum | solution.py:81
  137.0 0.1 fusion.31
  137.2 0.3 copy-done
  137.5 1.4 convolution_convert_fusion
  138.9 0.0 all-reduce.2.cloned.1.call-update
  139.0 42.2 %all-reduce.2.cloned.1.call-done = bf16[32,2560]{1,0:T(8,128)(2,1)} async-done(((bf16[32,2560]{1,0:T(8,128)(2,1)}), bf16[32,2560]{1,0:T(8,128)(2,1)}) %all-reduce.2.cloned.1.call-update) | async-done | bytes 163856 | tf_op jit(solution)/shard_map/psum | solution.py:101
  181.2 1.4 add_convert_fusion
  (21 shorter events, 0.2 us)
Async XLA Ops:
  6.5 10.4 %copy-start.3 = (s32[1024]{0:T(1024)S(1)}, s32[1024]{0:T(1024)}, u32[]{:S(2)}) copy-start(s32[1024]{0:T(1024)} %param.13) | copy-start | bytes 12292
  6.5 11.0 %copy-start.6 = (s32[64]{0:T(128)S(1)}, s32[64]{0:T(128)}, u32[]{:S(2)}) copy-start(s32[64]{0:T(128)} %param.15) | copy-start | bytes 772
  6.5 11.2 %copy-start.5 = (s32[1024]{0:T(1024)S(1)}, s32[1024]{0:T(1024)}, u32[]{:S(2)}) copy-start(s32[1024]{0:T(1024)} %param.14) | copy-start | bytes 12292
  8.7 31.4 %all-to-all-start = ((bf16[32,32,768]{2,1,0:T(8,128)(2,1)}), bf16[32,32,768]{2,1,0:T(8,128)(2,1)S(1)}, u32[]{:S(2)}, u32[]{:S(2)}) async-start(bf16[32,32,768]{2,1,0:T(8,128)(2,1)} %stack.2), calls=%async_computation | async-start | bytes 3145728 | tf_op jit(solution)/shard_map/all_to_all | solution.py:46
  52.8 11.4 %all-to-all-start.3 = ((f32[32,32,3]{1,2,0:T(4,128)}), f32[32,32,3]{1,2,0:T(4,128)S(1)}, u32[]{:S(2)}, u32[]{:S(2)}) async-start(f32[32,32,3]{1,2,0:T(4,128)} %copy.63), calls=%async_computation.3 | async-start | bytes 131072 | tf_op jit(solution)/shard_map/all_to_all | solution.py:71
  64.2 11.4 %all-to-all-start.2 = ((f32[32,32,3]{1,2,0:T(4,128)}), f32[32,32,3]{1,2,0:T(4,128)S(1)}, u32[]{:S(2)}, u32[]{:S(2)}) async-start(f32[32,32,3]{1,2,0:T(4,128)} %copy.59), calls=%async_computation.2 | async-start | bytes 131072 | tf_op jit(solution)/shard_map/all_to_all | solution.py:70
  73.7 7.7 %copy-start.1 = (bf16[32,768]{1,0:T(8,128)(2,1)S(1)}, bf16[32,768]{1,0:T(8,128)(2,1)}, u32[]{:S(2)}) copy-start(bf16[32,768]{1,0:T(8,128)(2,1)} %param.9) | copy-start | bytes 147460
  73.7 7.7 %copy-start.4 = (bf16[32,512]{1,0:T(8,128)(2,1)S(1)}, bf16[32,512]{1,0:T(8,128)(2,1)}, u32[]{:S(2)}) copy-start(bf16[32,512]{1,0:T(8,128)(2,1)} %param.10) | copy-start | bytes 98308
  75.6 58.5 %all-to-all-start.1 = ((f32[1024,3,256]{2,1,0:T(4,128)}), f32[1024,3,256]{2,1,0:T(4,128)}, u32[]{:S(2)}, u32[]{:S(2)}) async-start(f32[1024,3,256]{2,1,0:T(4,128)} %copy.57), calls=%async_computation.1 | async-start | bytes 8388608 | tf_op jit(solution)/shard_map/all_to_all | solution.py:72
  81.3 99.8 %all-reduce.2.cloned.1.call-start = ((), (), s32[]{:S(2)}) async-start(), calls=%async_computation.4 | async-start | bytes 327680 | tf_op jit(solution)/shard_map/psum | solution.py:101
  134.1 3.4 %copy-start = (bf16[768,2560]{1,0:T(8,128)(2,1)S(1)}, bf16[768,2560]{1,0:T(8,128)(2,1)}, u32[]{:S(2)}) copy-start(bf16[768,2560]{1,0:T(8,128)(2,1)} %param.12) | copy-start | bytes 11796484
  134.1 47.1 %copy-start.2 = (bf16[32,640]{1,0:T(8,128)(2,1)S(1)}, bf16[32,640]{1,0:T(8,128)(2,1)}, u32[]{:S(2)}) copy-start(bf16[32,640]{1,0:T(8,128)(2,1)} %param.8) | copy-start | bytes 122884
Sparse Core Ops, SparseCore 0:
  139.1 42.0 all-reduce.1
